TPU v7x, 512 devices: a whole 4x4x16 slice. The times are simulated.
512 devices in a mesh: src: 64 (over z, x), tm: 8 (over y, core).
Axes of the slice: x: 4, y: 4, z: 16, core: 2. Of those that a mesh axis runs over, the one named last changes fastest.
Arguments:
- left_vector: float32 [8, 131072], P(None, ('src', 'tm')), may hold values from -12 to 12
- source_coeffs: float32 [5, 8, 131072], P(None, None, ('src', 'tm')), may hold values from -1.5 to 1.5
- knot_coeffs: float32 [12, 8, 131072], P(None, None, ('src', 'tm')), may hold values from -1.5 to 1.5
- source_index: int32 [8, 131072], P(None, ('src', 'tm')), may hold values from 0 to 1023
- band_start: int32 [8, 131072], P(None, ('src', 'tm')), may hold values from 0 to 4095, as said below
- bucket_fill: int32 [8, 512], P(None, ('src', 'tm')), may hold values from 51 to 256, as said below
- source_vector: float32 [5, 524288], P(None, ('src', 'tm')), may hold values from -6 to 6
- knot_vector: float32 [3, 8, 16384], P(None, 'tm', 'src'), may hold values from -6 to 6
- source_search: float32 [5, 524288], P(None, ('src', 'tm')), may hold values from -6 to 6
- knot_search: float32 [3, 8, 16384], P(None, 'tm', 'src'), may hold values from -6 to 6
- source_solution: float32 [5, 524288], P(None, ('src', 'tm')), may hold values from -6 to 6
- knot_solution: float32 [3, 8, 16384], P(None, 'tm', 'src'), may hold values from -6 to 6
- recurrence: float32 [3], replicated, may hold values from 0.5 to 1.5
Outputs:
- left_next: float32 [8, 131072], P(None, ('src', 'tm'))
- source_next: float32 [5, 524288], P(None, ('src', 'tm'))
- knot_next: float32 [3, 8, 16384], P(None, 'tm', 'src')
- search_source: float32 [5, 524288], P(None, ('src', 'tm'))
- search_knot: float32 [3, 8, 16384], P(None, 'tm', 'src')
- solution_source: float32 [5, 524288], P(None, ('src', 'tm'))
- solution_knot: float32 [3, 8, 16384], P(None, 'tm', 'src')
- recurrence_next: float32 [4], replicated
Inputs may be any that keep to these rules, and one draw needn't show every extreme that they name: `bucket_fill`: in every draw one bucket of some group block holds exactly 256 observations. Call band_start // 64 the knot owner of a slot. Among the 8 x 256 slots of one column block of 256, each knot owner is named at most 64 times, and in every block some owner exactly 64 times.
All inputs are finite; a program needn't handle non-finite values.
Results may differ from a plain program's by a relative error of at most 0.00002.
Values sent between devices are 32-bit elements; how exact they have to be, the bound alone decides.
A program may use at most 64 MiB of HBM per device.

v0:
```python
import jax
import jax.numpy as jnp
from jax import lax
from jax.sharding import PartitionSpec as P

KB = 4
EPSILON = 1e-06


def band_positions(band_start, knots_slab):
    rows = jnp.arange(3 * KB, dtype=jnp.int32)
    base = rows // KB * knots_slab + rows % KB
    return base[:, None, None] + KB * band_start[None]


def shards(
    left_vector,
    source_coeffs,
    knot_coeffs,
    source_index,
    band_start,
    bucket_fill,
    source_vector,
    knot_vector,
    source_search,
    knot_search,
    source_solution,
    knot_solution,
    recurrence,
):
    slab_count = lax.axis_size("tm")
    group_count = lax.axis_size("src")
    devices = slab_count * group_count
    buckets, capacity = left_vector.shape
    source_dev = source_vector.shape[1]
    knot_dev = knot_vector.shape[2]
    knots_slab = knot_dev * group_count
    total_obs = buckets * capacity * devices
    unknowns = (5 * source_dev + 3 * knot_dev) * devices
    ratio = unknowns / total_obs
    alpha = recurrence[0]
    pivot = recurrence[1]
    remainder = recurrence[2]
    slot = lax.broadcasted_iota(jnp.int32, (buckets, capacity), 1)
    valid = (slot < bucket_fill).astype(jnp.float32)
    flat_source = source_index.reshape(-1)
    picked = jnp.take(source_vector, flat_source, axis=1).reshape(5, buckets, capacity)
    image = jnp.sum(source_coeffs * picked, axis=0)
    own_knots = knot_vector[:, 0, :]
    slab_whole = lax.all_gather(own_knots, "src", axis=1, tiled=True).reshape(-1)
    positions = band_positions(band_start, knots_slab)
    knot_image = jnp.sum(knot_coeffs * jnp.take(slab_whole, positions), axis=0)
    returned = lax.all_to_all(knot_image, "tm", split_axis=0, concat_axis=0, tiled=True)
    raw = valid * (image + returned - alpha * left_vector)
    own_squares = jnp.sum(raw * raw)
    beta = jnp.sqrt(lax.psum(own_squares, ("src", "tm")) / total_obs + EPSILON)
    outgoing = raw / beta
    arrived = lax.all_to_all(outgoing, "tm", split_axis=0, concat_axis=0, tiled=True)
    gradient_source = (
        jnp.zeros((5, source_dev), jnp.float32)
        .at[:, flat_source]
        .add((source_coeffs * outgoing[None]).reshape(5, -1))
    )
    knot_terms = (
        jnp.zeros((3 * knots_slab,), jnp.float32)
        .at[positions.reshape(-1)]
        .add((knot_coeffs * arrived[None]).reshape(-1))
        .reshape(3, knots_slab)
    )
    knot_totals = lax.psum(knot_terms, "src")
    gradient_knot = lax.dynamic_slice_in_dim(
        knot_totals, lax.axis_index("src") * knot_dev, knot_dev, 1
    )
    source_raw = ratio * gradient_source - beta * source_vector
    knot_raw = ratio * gradient_knot - beta * own_knots
    squares = jnp.sum(source_raw * source_raw) + jnp.sum(knot_raw * knot_raw)
    alpha_next = jnp.sqrt(lax.psum(squares, ("src", "tm")) / unknowns + EPSILON)
    left_next = raw / beta
    source_next = source_raw / alpha_next
    knot_next = knot_raw / alpha_next
    radius = jnp.sqrt(pivot * pivot + beta * beta)
    cosine = pivot / radius
    sine = beta / radius
    coupling = sine * alpha_next
    step_gain = cosine * remainder
    solution_source = source_solution + step_gain / radius * source_search
    solution_knot = knot_solution + step_gain / radius * knot_search
    search_source = source_next - coupling / radius * source_search
    search_knot = knot_next[:, None, :] - coupling / radius * knot_search
    recurrence_next = jnp.stack([alpha_next, beta, -cosine * alpha_next, sine * remainder])
    return (
        left_next,
        source_next,
        knot_next[:, None, :],
        search_source,
        search_knot,
        solution_source,
        solution_knot,
        recurrence_next,
    )


def solution(mesh):
    in_specs = (
        P(None, ("src", "tm")),
        P(None, None, ("src", "tm")),
        P(None, None, ("src", "tm")),
        P(None, ("src", "tm")),
        P(None, ("src", "tm")),
        P(None, ("src", "tm")),
        P(None, ("src", "tm")),
        P(None, "tm", "src"),
        P(None, ("src", "tm")),
        P(None, "tm", "src"),
        P(None, ("src", "tm")),
        P(None, "tm", "src"),
        P(),
    )
    out_specs = (
        P(None, ("src", "tm")),
        P(None, ("src", "tm")),
        P(None, "tm", "src"),
        P(None, ("src", "tm")),
        P(None, "tm", "src"),
        P(None, ("src", "tm")),
        P(None, "tm", "src"),
        P(),
    )
    return jax.shard_map(shards, mesh=mesh, in_specs=in_specs, out_specs=out_specs, check_vma=False)
```

profile of v0, /device:TPU:1, one launch (start us, length us, event | category | flops | bytes accessed | tf_op | source)
XLA Modules:
  0.0 866.1 jit_solution(7644518561160794615)
XLA Ops:
  7.2 71.3 %all-gather = f32[3,1,16384]{2,1,0:T(1,128)S(1)} all-gather(f32[3,1,256]{2,1,0:T(1,128)} %param.20), channel_id=2, replica_groups=mesh['src'=64,'tm'=8] {'src'}, dimensions={2}, use_global_device_ids=true | all-gather | bytes 199680 | tf_op jit(solution)/shard_map/all_gather | solution.py:50
  78.7 135.5 %gather_fusion.1 = f32[24576]{0:T(1024)S(1)} fusion(f32[49152]{0:T(1024)S(1)} %bitcast.46, s32[24576]{0:T(1024)S(1)} %broadcast_clamp_fusion), kind=kCustom, calls=%fused_computation.1 | custom fusion | bytes 294912 | tf_op jit(solution)/shard_map/jit(_take)/gather | solution.py:52
  214.3 0.8 copy-done
  215.2 0.6 all_to_all.14
  215.8 23.8 %all-to-all-start = ((f32[8,1,256]{2,1,0:T(1,128)}), f32[8,1,256]{2,1,0:T(1,128)S(1)}, u32[]{:S(2)}, u32[]{:S(2)}) async-start(f32[8,1,256]{2,1,0:T(1,128)} %all_to_all.14), calls=%async_computation | async-start | bytes 16384 | tf_op jit(solution)/shard_map/all_to_all | solution.py:53
  239.7 0.7 copy-done.1
  240.4 0.2 copy.52
  240.6 0.5 copy-done.5
  241.2 5.5 gather_fusion
  246.7 0.3 copy.53
  247.2 0.7 copy-done.2
  247.9 0.6 fusion.10
  249.8 0.7 copy-done.9
  250.5 1.3 multiply_reduce_fusion.3
  251.8 101.1 %psum.21 = f32[]{:T(128)} all-reduce(f32[]{:T(128)} %get-tuple-element.34), channel_id=1, replica_groups=mesh['src'=64,'tm'=8] {'src','tm'}, use_global_device_ids=true, to_apply=%region_3.4 | all-reduce | flops 1 | bytes 8 | tf_op jit(solution)/shard_map/psum | solution.py:56
  353.6 0.6 copy.56
  354.2 4.0 all-to-all-start.1
  358.2 4.6 all-to-all-done.1
  362.9 128.4 %scatter_custom_fusion.1 = f32[49152]{0:T(1024)S(1)} fusion(s32[24576]{0:T(1024)S(1)} %bitcast.50, f32[24576]{0:T(1024)S(1)} %bitcast.51, f32[]{:T(128)} %constant.77.clone.1), kind=kCustom, calls=%fused_computation.11 | custom fusion | flops 24576 | bytes 196612 | tf_op jit(solution)/shard_map/scatter-add | solution.py:67
  491.3 0.8 reshape.152
  492.9 0.4 copy.58
  493.3 11.6 %scatter_custom_fusion = f32[5,1024]{0,1:T(8,128)S(1)} fusion(s32[2048]{0:T(1024)S(1)} %bitcast.55, f32[2048,5]{1,0:T(8,128)S(1)} %bitcast.48, f32[]{:T(128)} %constant.77.clone.1), kind=kCustom, calls=%fused_computation.7 | custom fusion | flops 10240 | bytes 20484 | tf_op jit(solution)/shard_map/scatter-add | solution.py:62
  504.9 0.2 copy.55
  505.8 0.6 multiply_reduce_fusion.2
  506.4 236.0 %all-reduce.2.cloned.1.call-done = f32[3,16384]{1,0:T(4,128)} async-done(((f32[3,16384]{1,0:T(4,128)}), f32[3,16384]{1,0:T(4,128)}) %all-reduce.2.cloned.1.call-update) | async-done | bytes 196624 | tf_op jit(solution)/shard_map/psum | solution.py:70
  742.4 1.3 multiply_reduce_fusion.4
  745.6 109.7 %psum.23 = f32[]{:T(128)} all-reduce(f32[]{:T(128)S(6)} %add.179), channel_id=1, replica_groups=mesh['src'=64,'tm'=8] {'src','tm'}, use_global_device_ids=true, to_apply=%region_9.10 | all-reduce | flops 1 | bytes 8 | tf_op jit(solution)/shard_map/psum | solution.py:77
  856.1 0.7 broadcast_divide_fusion.2
  856.8 0.6 broadcast_in_dim.37
  857.4 0.7 multiply_subtract_fusion
  858.1 0.6 multiply_add_fusion.1
  858.7 0.6 pad_maximum_fusion
  (47 shorter events, 0.8 us)
Async XLA Ops:
  7.2 71.3 %copy-start.8 = (s32[8,256]{1,0:T(8,128)S(1)}, s32[8,256]{1,0:T(8,128)}, u32[]{:S(2)}) copy-start(s32[8,256]{1,0:T(8,128)} %param.17) | copy-start | bytes 24580
  214.2 0.9 copy-start
  215.8 34.0 %all-to-all-start = ((f32[8,1,256]{2,1,0:T(1,128)}), f32[8,1,256]{2,1,0:T(1,128)S(1)}, u32[]{:S(2)}, u32[]{:S(2)}) async-start(f32[8,1,256]{2,1,0:T(1,128)} %all_to_all.14), calls=%async_computation | async-start | bytes 16384 | tf_op jit(solution)/shard_map/all_to_all | solution.py:53
  239.7 0.8 copy-start.1
  240.4 0.7 copy-start.5
  246.7 1.3 copy-start.10
  247.1 0.8 copy-start.2
  249.8 0.7 copy-start.9
  249.8 0.7 copy-start.13
  354.2 8.6 all-to-all-start.1
  358.2 384.2 %all-reduce.2.cloned.1.call-start = ((), (), s32[]{:S(2)}) async-start(), calls=%async_computation.2 | async-start | bytes 524288 | tf_op jit(solution)/shard_map/psum | solution.py:70
  358.2 134.0 %copy-start.6 = (f32[8,256]{1,0:T(8,128)}, f32[8,256]{1,0:T(8,128)S(1)}, u32[]{:S(2)}) copy-start(f32[8,256]{1,0:T(8,128)S(1)} %broadcast_divide_fusion.1) | copy-start | bytes 24580
  505.8 236.6 %copy-start.7 = (f32[3,1,256]{2,1,0:T(1,128)S(1)}, f32[3,1,256]{2,1,0:T(1,128)}, u32[]{:S(2)}) copy-start(f32[3,1,256]{2,1,0:T(1,128)} %param.20) | copy-start | bytes 9220
  505.8 351.6 %copy-start.4 = (f32[5,1024]{1,0:T(8,128)S(1)}, f32[5,1024]{1,0:T(8,128)}, u32[]{:S(2)}) copy-start(f32[5,1024]{1,0:T(8,128)} %param.23) | copy-start | bytes 61444
  506.4 351.0 %copy-start.3 = (f32[5,1024]{1,0:T(8,128)S(1)}, f32[5,1024]{1,0:T(8,128)}, u32[]{:S(2)}) copy-start(f32[5,1024]{1,0:T(8,128)} %param.21) | copy-start | bytes 61444
  857.4 0.7 copy-start.11
  857.4 0.7 copy-start.12
Sparse Core Ops, SparseCore 0:
  492.3 250.0 all-reduce.1
where the time goes:
time: 867 us; the launch traced here: 866 us
  blocking collectives  282 us (33%)
  waiting for transfers between devices  241 us (28%)
  local copies, waits for them, and re-layouts  149 us (17%)
  other arithmetic  146 us (17%)
  starting transfers between devices  27.8 us (3%)
  between operations  20.4 us (2%)
    psum x1, waiting for transfers between devices, shards(): knot_totals = lax.psum(knot_terms, 'src')  236 us
    gather x2, local copies, waits for them, and re-layouts, shards(): knot_image = jnp.sum(knot_coeffs * jnp.take(slab_whole, positions), axis=0)  136 us
    scatter-add x1, other arithmetic, shards(): knot_terms = jnp.zeros((3 * knots_slab,), jnp.float32).at[positions.resha...  128 us
    psum x1, blocking collectives, shards(): alpha_next = jnp.sqrt(lax.psum(squares, ('src', 'tm')) / unknowns + EPSILON)  110 us
    psum x1, blocking collectives, shards(): beta = jnp.sqrt(lax.psum(own_squares, ('src', 'tm')) / total_obs + EPSILON)  101 us
    all_gather x1, blocking collectives, shards(): lax.all_gather(own_knots, 'src', axis=1, tiled=True).reshape(-1)  71.3 us
    all_to_all x1, starting transfers between devices, shards(): lax.all_to_all(knot_image, 'tm', split_axis=0, concat_axis=0, tiled=True)  23.8 us
  transfers between devices with their start and end apart: 3, of which 2 were waited for; matrix products, arithmetic and copies ran while one was open for 2% of the time, Pallas kernels for 0%

commit v1 on v0

--- a/solution.py
+++ b/solution.py
@@ -5,6 +5,11 @@
 
 KB = 4
 EPSILON = 1e-06
+
+
+def gather_from_all(shard, axis, dim):
+    copies = jnp.concatenate([shard] * lax.axis_size(axis), axis=dim)
+    return lax.all_to_all(copies, axis, dim, dim, tiled=True)
 
 
 def band_positions(band_start, knots_slab):
@@ -47,7 +52,7 @@
     picked = jnp.take(source_vector, flat_source, axis=1).reshape(5, buckets, capacity)
     image = jnp.sum(source_coeffs * picked, axis=0)
     own_knots = knot_vector[:, 0, :]
-    slab_whole = lax.all_gather(own_knots, "src", axis=1, tiled=True).reshape(-1)
+    slab_whole = gather_from_all(own_knots, "src", 1).reshape(-1)
     positions = band_positions(band_start, knots_slab)
     knot_image = jnp.sum(knot_coeffs * jnp.take(slab_whole, positions), axis=0)
     returned = lax.all_to_all(knot_image, "tm", split_axis=0, concat_axis=0, tiled=True)

time: 867 us -> 811 us (0.935)
  blocking collectives: 282 us -> 209 us
  waiting for transfers between devices: 241 us -> 252 us
    all_gather x1 -> x0, blocking collectives: 71.3 us -> none  [shards(): lax.all_gather(own_knots, 'src', axis=1, tiled=True).reshape(-1)]
    all_to_all x0 -> x1, starting transfers between devices: none -> 19.2 us  [gather_from_all(): return lax.all_to_all(copies, axis, dim, dim, tiled=True)]
    all_to_all x1, starting transfers between devices: 23.8 us -> 8.38 us  [shards(): lax.all_to_all(knot_image, 'tm', split_axis=0, concat_axis=0, tiled=True)]
    all_to_all x0 -> x1, waiting for transfers between devices: none -> 11.1 us  [gather_from_all(): return lax.all_to_all(copies, axis, dim, dim, tiled=True)]
  transfers between devices with their start and end apart: 3 -> 4, of which waited for: 2 -> 4; matrix products, arithmetic and copies ran while one was open for 2% -> 2% of each run, Pallas kernels for 0% -> 0%
where the time goes in v1:
time: 811 us; the launch traced here: 810 us
  waiting for transfers between devices  252 us (31%)
  blocking collectives  209 us (26%)
  local copies, waits for them, and re-layouts  150 us (18%)
  other arithmetic  146 us (18%)
  starting transfers between devices  31.5 us (4%)
  between operations  20.4 us (3%)
    psum x1, waiting for transfers between devices, shards(): knot_totals = lax.psum(knot_terms, 'src')  234 us
    gather x2, local copies, waits for them, and re-layouts, shards(): knot_image = jnp.sum(knot_coeffs * jnp.take(slab_whole, positions), axis=0)  136 us
    scatter-add x1, other arithmetic, shards(): knot_terms = jnp.zeros((3 * knots_slab,), jnp.float32).at[positions.resha...  128 us
    psum x1, blocking collectives, shards(): alpha_next = jnp.sqrt(lax.psum(squares, ('src', 'tm')) / unknowns + EPSILON)  110 us
    psum x1, blocking collectives, shards(): beta = jnp.sqrt(lax.psum(own_squares, ('src', 'tm')) / total_obs + EPSILON)  99.4 us
    all_to_all x1, starting transfers between devices, gather_from_all(): return lax.all_to_all(copies, axis, dim, dim, tiled=True)  19.2 us
  transfers between devices with their start and end apart: 4, of which 4 were waited for; matrix products, arithmetic and copies ran while one was open for 2% of the time, Pallas kernels for 0%

profile of v1, /device:TPU:1, one launch (start us, length us, event | category | flops | bytes accessed | tf_op | source)
XLA Modules:
  0.0 809.8 jit_solution(12406862966683188085)
XLA Ops:
  7.2 0.7 copy.85
  7.9 0.7 concatenate.4
  8.6 19.2 %all-to-all-start = ((f32[3,64,256]{2,0,1:T(4,128)}), f32[3,64,256]{2,0,1:T(4,128)S(1)}, u32[]{:S(2)}, u32[]{:S(2)}) async-start(f32[3,64,256]{2,0,1:T(4,128)} %concatenate.4), calls=%async_computation | async-start | bytes 524288 | tf_op jit(solution)/shard_map/all_to_all | solution.py:12
  28.0 0.7 copy-done.1
  28.9 0.5 copy-done.5
  29.5 5.5 gather_fusion
  35.6 0.7 copy-done.2
  36.2 11.1 %all-to-all-done = f32[3,64,256]{2,0,1:T(4,128)S(1)} async-done(((f32[3,64,256]{2,0,1:T(4,128)}), f32[3,64,256]{2,0,1:T(4,128)S(1)}, u32[]{:S(2)}, u32[]{:S(2)}) %all-to-all-start) | async-done | bytes 196640 | tf_op jit(solution)/shard_map/all_to_all | solution.py:12
  47.5 135.5 %gather_fusion.1 = f32[24576]{0:T(1024)S(1)} fusion(f32[49152]{0:T(1024)S(1)} %bitcast.50, s32[24576]{0:T(1024)S(1)} %broadcast_clamp_fusion), kind=kCustom, calls=%fused_computation.1 | custom fusion | bytes 294912 | tf_op jit(solution)/shard_map/jit(_take)/gather | solution.py:57
  183.1 0.8 copy-done
  184.0 0.6 all_to_all.19
  184.6 8.4 %all-to-all-start.1 = ((f32[8,1,256]{2,1,0:T(1,128)}), f32[8,1,256]{2,1,0:T(1,128)S(1)}, u32[]{:S(2)}, u32[]{:S(2)}) async-start(f32[8,1,256]{2,1,0:T(1,128)} %all_to_all.19), calls=%async_computation.1 | async-start | bytes 16384 | tf_op jit(solution)/shard_map/all_to_all | solution.py:58
  193.0 0.6 fusion.10
  194.9 2.7 all-to-all-done.1
  197.6 0.7 copy-done.13
  198.3 1.3 multiply_reduce_fusion.3
  199.6 99.4 %psum.21 = f32[]{:T(128)} all-reduce(f32[]{:T(128)} %get-tuple-element.42), channel_id=1, replica_groups=mesh['src'=64,'tm'=8] {'src','tm'}, use_global_device_ids=true, to_apply=%region_3.4 | all-reduce | flops 1 | bytes 8 | tf_op jit(solution)/shard_map/psum | solution.py:61
  299.7 0.6 copy.65
  300.3 3.9 all-to-all-start.2
  304.2 4.6 all-to-all-done.2
  308.9 128.4 %scatter_custom_fusion.1 = f32[49152]{0:T(1024)S(1)} fusion(s32[24576]{0:T(1024)S(1)} %bitcast.55, f32[24576]{0:T(1024)S(1)} %bitcast.56, f32[]{:T(128)} %constant.77.clone.1), kind=kCustom, calls=%fused_computation.11 | custom fusion | flops 24576 | bytes 196612 | tf_op jit(solution)/shard_map/scatter-add | solution.py:72
  437.4 0.8 reshape.284
  439.3 11.6 %scatter_custom_fusion = f32[5,1024]{0,1:T(8,128)S(1)} fusion(s32[2048]{0:T(1024)S(1)} %bitcast.60, f32[2048,5]{1,0:T(8,128)S(1)} %bitcast.52, f32[]{:T(128)} %constant.77.clone.1), kind=kCustom, calls=%fused_computation.7 | custom fusion | flops 10240 | bytes 20484 | tf_op jit(solution)/shard_map/scatter-add | solution.py:67
  451.9 0.6 multiply_reduce_fusion.2
  452.5 233.6 %all-reduce.2.cloned.1.call-done = f32[3,16384]{1,0:T(4,128)} async-done(((f32[3,16384]{1,0:T(4,128)}), f32[3,16384]{1,0:T(4,128)}) %all-reduce.2.cloned.1.call-update) | async-done | bytes 196624 | tf_op jit(solution)/shard_map/psum | solution.py:75
  686.0 1.3 multiply_reduce_fusion.4
  689.3 109.7 %psum.23 = f32[]{:T(128)} all-reduce(f32[]{:T(128)S(6)} %add.179), channel_id=1, replica_groups=mesh['src'=64,'tm'=8] {'src','tm'}, use_global_device_ids=true, to_apply=%region_9.10 | all-reduce | flops 1 | bytes 8 | tf_op jit(solution)/shard_map/psum | solution.py:82
  799.8 0.7 broadcast_divide_fusion.2
  800.4 0.6 broadcast_in_dim.37
  801.0 0.7 multiply_subtract_fusion
  801.7 0.6 multiply_add_fusion.1
  802.3 0.6 pad_maximum_fusion
  (52 shorter events, 2.0 us)
Async XLA Ops:
  8.6 19.3 %copy-start.8 = (s32[8,256]{1,0:T(8,128)S(1)}, s32[8,256]{1,0:T(8,128)}, u32[]{:S(2)}) copy-start(s32[8,256]{1,0:T(8,128)} %param.17) | copy-start | bytes 24580
  8.6 38.7 %all-to-all-start = ((f32[3,64,256]{2,0,1:T(4,128)}), f32[3,64,256]{2,0,1:T(4,128)S(1)}, u32[]{:S(2)}, u32[]{:S(2)}) async-start(f32[3,64,256]{2,0,1:T(4,128)} %concatenate.4), calls=%async_computation | async-start | bytes 524288 | tf_op jit(solution)/shard_map/all_to_all | solution.py:12
  27.9 0.8 copy-start.1
  28.7 0.7 copy-start.5
  35.4 0.8 copy-start.2
  47.5 145.6 %copy-start.10 = (f32[3]{0:T(128)S(1)}, f32[3]{0:T(128)}, u32[]{:S(2)}) copy-start(f32[3]{0:T(128)} %param.25) | copy-start | bytes 40
  183.0 0.9 copy-start
  184.6 13.0 %all-to-all-start.1 = ((f32[8,1,256]{2,1,0:T(1,128)}), f32[8,1,256]{2,1,0:T(1,128)S(1)}, u32[]{:S(2)}, u32[]{:S(2)}) async-start(f32[8,1,256]{2,1,0:T(1,128)} %all_to_all.19), calls=%async_computation.1 | async-start | bytes 16384 | tf_op jit(solution)/shard_map/all_to_all | solution.py:58
  194.9 2.7 copy-start.9
  197.6 0.7 copy-start.13
  300.3 8.5 %all-to-all-start.2 = ((f32[8,1,256]{2,1,0:T(1,128)}), f32[8,1,256]{2,1,0:T(1,128)S(1)}, u32[]{:S(2)}, u32[]{:S(2)}) async-start(f32[8,1,256]{2,1,0:T(1,128)} %copy.65), calls=%async_computation.2 | async-start | bytes 16384 | tf_op jit(solution)/shard_map/all_to_all | solution.py:63
  304.2 381.8 %all-reduce.2.cloned.1.call-start = ((), (), s32[]{:S(2)}) async-start(), calls=%async_computation.3 | async-start | bytes 524288 | tf_op jit(solution)/shard_map/psum | solution.py:75
  304.2 134.0 %copy-start.6 = (f32[8,256]{1,0:T(8,128)}, f32[8,256]{1,0:T(8,128)S(1)}, u32[]{:S(2)}) copy-start(f32[8,256]{1,0:T(8,128)S(1)} %broadcast_divide_fusion.1) | copy-start | bytes 24580
  451.8 234.2 %copy-start.7 = (f32[3,1,256]{2,1,0:T(1,128)S(1)}, f32[3,1,256]{2,1,0:T(1,128)}, u32[]{:S(2)}) copy-start(f32[3,1,256]{2,1,0:T(1,128)} %param.20) | copy-start | bytes 9220
  451.8 349.2 %copy-start.4 = (f32[5,1024]{1,0:T(8,128)S(1)}, f32[5,1024]{1,0:T(8,128)}, u32[]{:S(2)}) copy-start(f32[5,1024]{1,0:T(8,128)} %param.23) | copy-start | bytes 61444
  452.5 348.6 %copy-start.3 = (f32[5,1024]{1,0:T(8,128)S(1)}, f32[5,1024]{1,0:T(8,128)}, u32[]{:S(2)}) copy-start(f32[5,1024]{1,0:T(8,128)} %param.21) | copy-start | bytes 61444
  801.0 0.7 copy-start.11
  801.0 0.7 copy-start.12
Sparse Core Ops, SparseCore 0:
  438.3 247.6 all-reduce.1
